TPU v7x, 32 devices: a whole 2x2x4 slice. The times are simulated.
32 devices in a mesh: dp: 16 (over z, y, core), mp: 2 (over x).
Axes of the slice: x: 2, y: 2, z: 4, core: 2. Of those that a mesh axis runs over, the one named last changes fastest.
Arguments:
- layer_input: bfloat16 [24576, 768], P(('dp', 'mp')), may hold values from -6 to 6
- gain_attn: bfloat16 [768], replicated, may hold values from 0.5 to 1.5
- w_query: bfloat16 [768, 768], P(None, 'mp'), may hold values from -0.3125 to 0.3125
- w_key: bfloat16 [768, 768], P(None, 'mp'), may hold values from -0.21875 to 0.21875
- w_value: bfloat16 [768, 768], P(None, 'mp'), may hold values from -0.21875 to 0.21875
- w_out: bfloat16 [768, 768], P('mp'), may hold values from -0.875 to 0.875
- gain_mlp: bfloat16 [768], replicated, may hold values from 0.5 to 1.5
- w_gate: bfloat16 [768, 2048], P(None, 'mp'), may hold values from -0.21875 to 0.21875
- w_up: bfloat16 [768, 2048], P(None, 'mp'), may hold values from -0.21875 to 0.21875
- w_down: bfloat16 [2048, 768], P('mp'), may hold values from -0.125 to 0.125
- segment_start: int32 [16, 7], P('dp'), may hold values from 0 to 1472, as said below
- segment_parent: int32 [16, 7], P('dp'), may hold values from 0 to 2, as said below
- out_grad: bfloat16 [24576, 768], P(('dp', 'mp')), may hold values from -6 to 6
Outputs:
- output: float32 [24576, 768], P(('dp', 'mp'))
- input_grad: float32 [24576, 768], P(('dp', 'mp'))
- gain_attn_grad: float32 [768], replicated
- w_query_grad: float32 [768, 768], P(None, 'mp')
- w_key_grad: float32 [768, 768], P(None, 'mp')
- w_value_grad: float32 [768, 768], P(None, 'mp')
- w_out_grad: float32 [768, 768], P('mp')
- gain_mlp_grad: float32 [768], replicated
- w_gate_grad: float32 [768, 2048], P(None, 'mp')
- w_up_grad: float32 [768, 2048], P(None, 'mp')
- w_down_grad: float32 [2048, 768], P('mp')
Inputs may be any that keep to these rules, and one draw needn't show every extreme that they name: `segment_start`: per tree the segments are stored in order trunk, two branches, four leaves; starts rise strictly from 0, every branch or leaf has 64 to 192 tokens, and the last leaf has exactly 64. `segment_parent`: segment 0 is the trunk (entry 0), segments 1 and 2 have parent 0, and each of them is the parent of exactly two of segments 3 to 6.
All inputs are finite; a program needn't handle non-finite values.
Results may differ from a plain program's by a relative error of at most 0.018.
Values may be sent and summed in bfloat16 or wider, within the bound.
A program may use at most 192 MiB of HBM per device.

v0:
```python
import jax
import jax.numpy as jnp
from jax import lax
from jax.sharding import PartitionSpec as P

HD = 64
EPSILON = 1e-05
ROPE_BASE = 10000.0


def tree_tables(starts, parents, length):
    seg_count = starts.shape[0]
    tok_index = jnp.arange(length, dtype=jnp.int32)
    labels = jnp.arange(seg_count, dtype=jnp.int32)
    segment = jnp.sum(
        (tok_index[:, None] >= starts[None, 1:]).astype(jnp.int32), axis=1, dtype=jnp.int32
    )
    seg_ends = jnp.concatenate([starts[1:], jnp.full((1,), length, dtype=jnp.int32)])
    seg_lengths = seg_ends - starts
    same_seg = (labels[:, None] == labels[None, :]).astype(jnp.int32)
    parent_hot = (parents[:, None] == labels[None, :]).astype(jnp.int32)
    reaches = same_seg + parent_hot + jnp.dot(parent_hot, parent_hot)
    ancestry = (reaches > 0).astype(jnp.int32)
    offset = jnp.dot(ancestry * (1 - same_seg), seg_lengths)
    onehot = (segment[:, None] == labels[None, :]).astype(jnp.int32)
    position = tok_index - jnp.dot(onehot, starts) + jnp.dot(onehot, offset)
    visible = jnp.dot(onehot, ancestry)
    return (position, visible, onehot)


def rotary_tables(position, head_size):
    half_size = head_size // 2
    inv_freq = ROPE_BASE ** (-2.0 * jnp.arange(half_size, dtype=jnp.float32) / head_size)
    angles = position.astype(jnp.float32)[:, None] * inv_freq[None, :]
    return (jnp.cos(angles), jnp.sin(angles))


def rotate(vectors, cosine, sine_tab):
    half_size = vectors.shape[-1] // 2
    first_half = vectors[..., :half_size]
    second = vectors[..., half_size:]
    cos_b = cosine[:, None, :]
    sin_b = sine_tab[:, None, :]
    return jnp.concatenate(
        [first_half * cos_b - second * sin_b, second * cos_b + first_half * sin_b], axis=-1
    )


def rotate_back(gradient, cosine, sine_tab):
    half_size = gradient.shape[-1] // 2
    first_half = gradient[..., :half_size]
    second = gradient[..., half_size:]
    cos_b = cosine[:, None, :]
    sin_b = sine_tab[:, None, :]
    return jnp.concatenate(
        [first_half * cos_b + second * sin_b, second * cos_b - first_half * sin_b], axis=-1
    )


def contract_last(left_mat, right_mat):
    return lax.dot_general(
        left_mat, right_mat, (((1,), (1,)), ((), ())), preferred_element_type=jnp.float32
    )


def inner_rows(left_mat, right_mat):
    return lax.dot_general(
        left_mat, right_mat, (((0,), (0,)), ((), ())), preferred_element_type=jnp.float32
    )


def rms_scale(vectors):
    return lax.rsqrt(jnp.mean(vectors * vectors, axis=-1, keepdims=True) + EPSILON)


def on_device(
    layer_input,
    gain_attn,
    w_query,
    w_key,
    w_value,
    w_out,
    gain_mlp,
    w_gate,
    w_up,
    w_down,
    segment_start,
    segment_parent,
    out_grad,
):
    tok_rows = layer_input.shape[0]
    tree_len = tok_rows * lax.axis_size("mp")
    local_heads = w_query.shape[1] // HD
    score_scale = HD ** (-0.5)
    position, visible, onehot = tree_tables(segment_start[0], segment_parent[0], tree_len)
    cosine, sine_tab = rotary_tables(position, HD)
    block_rows = min(512, tree_len)
    block_starts = jnp.arange(tree_len // block_rows, dtype=jnp.int32) * block_rows
    key_index = jnp.arange(tree_len, dtype=jnp.int32)

    def block_mask(first_row):
        vis_block = lax.dynamic_slice_in_dim(visible, first_row, block_rows, 0)
        q_index = first_row + jnp.arange(block_rows, dtype=jnp.int32)
        return (jnp.dot(vis_block, onehot.T) > 0) & (key_index[None, :] <= q_index[:, None])

    inputs_f32 = layer_input.astype(jnp.float32)
    inv_one = rms_scale(inputs_f32)
    normed = (inputs_f32 * inv_one * gain_attn).astype(jnp.bfloat16)
    normed_all = lax.all_gather(normed, "mp", axis=0, tiled=True)
    q_pre = jnp.dot(normed_all, w_query, preferred_element_type=jnp.float32)
    k_pre = jnp.dot(normed_all, w_key, preferred_element_type=jnp.float32)
    values = jnp.dot(normed_all, w_value, preferred_element_type=jnp.float32).astype(jnp.bfloat16)
    values = values.reshape(tree_len, local_heads, HD)
    query = rotate(q_pre.reshape(tree_len, local_heads, HD), cosine, sine_tab).astype(jnp.bfloat16)
    key_rot = rotate(k_pre.reshape(tree_len, local_heads, HD), cosine, sine_tab).astype(
        jnp.bfloat16
    )

    def attend(first_row):
        q_block = lax.dynamic_slice_in_dim(query, first_row, block_rows, 0)
        scores = (
            jnp.einsum("qhd,khd->hqk", q_block, key_rot, preferred_element_type=jnp.float32)
            * score_scale
        )
        masked = jnp.where(block_mask(first_row)[None], scores, -1e30)
        row_max = jnp.max(masked, axis=-1, keepdims=True)
        exp_terms = jnp.exp(masked - row_max)
        row_sum = jnp.sum(exp_terms, axis=-1, keepdims=True)
        prob_rows = (exp_terms / row_sum).astype(jnp.bfloat16)
        head_out = jnp.einsum("hqk,khd->qhd", prob_rows, values, preferred_element_type=jnp.float32)
        return (head_out.astype(jnp.bfloat16), row_max[..., 0] + jnp.log(row_sum[..., 0]))

    head_blocks, lse_blocks = lax.map(attend, block_starts)
    heads_out = head_blocks.reshape(tree_len, local_heads * HD)
    attn_out = lax.psum_scatter(
        jnp.dot(heads_out, w_out, preferred_element_type=jnp.float32).astype(jnp.bfloat16),
        "mp",
        scatter_dimension=0,
        tiled=True,
    ).astype(jnp.float32)
    residual = inputs_f32 + attn_out
    inv_two = rms_scale(residual)
    normed_two = (residual * inv_two * gain_mlp).astype(jnp.bfloat16)
    normed_two_all = lax.all_gather(normed_two, "mp", axis=0, tiled=True)
    gate_pre = jnp.dot(normed_two_all, w_gate, preferred_element_type=jnp.float32)
    up_pre = jnp.dot(normed_two_all, w_up, preferred_element_type=jnp.float32)
    sigmoid_gate = jax.nn.sigmoid(gate_pre)
    silu_gate = gate_pre * sigmoid_gate
    hidden = (silu_gate * up_pre).astype(jnp.bfloat16)
    output = residual + lax.psum_scatter(
        jnp.dot(hidden, w_down, preferred_element_type=jnp.float32).astype(jnp.bfloat16),
        "mp",
        scatter_dimension=0,
        tiled=True,
    ).astype(jnp.float32)
    grads_all = lax.all_gather(out_grad, "mp", axis=0, tiled=True)
    grad_down = inner_rows(hidden, grads_all)
    d_hidden = contract_last(grads_all, w_down)
    d_gate = (d_hidden * up_pre * sigmoid_gate * (1.0 + gate_pre * (1.0 - sigmoid_gate))).astype(
        jnp.bfloat16
    )
    d_up = (d_hidden * silu_gate).astype(jnp.bfloat16)
    grad_gate = inner_rows(normed_two_all, d_gate)
    grad_up = inner_rows(normed_two_all, d_up)
    d_norm_two = lax.psum_scatter(
        (contract_last(d_gate, w_gate) + contract_last(d_up, w_up)).astype(jnp.bfloat16),
        "mp",
        scatter_dimension=0,
        tiled=True,
    ).astype(jnp.float32)
    scaled_two = gain_mlp * d_norm_two
    gain_mlp_part = jnp.sum(d_norm_two * residual * inv_two, axis=0)
    d_resid = (
        out_grad.astype(jnp.float32)
        + inv_two * scaled_two
        - residual * inv_two**3 * jnp.mean(scaled_two * residual, axis=-1, keepdims=True)
    )
    d_attn_all = lax.all_gather(d_resid.astype(jnp.bfloat16), "mp", axis=0, tiled=True)
    grad_out = inner_rows(heads_out, d_attn_all)
    d_heads = (
        contract_last(d_attn_all, w_out).astype(jnp.bfloat16).reshape(tree_len, local_heads, HD)
    )

    def attend_back(sums_in, block_items):
        key_acc, value_acc = sums_in
        first_row, lse_block = block_items
        q_block = lax.dynamic_slice_in_dim(query, first_row, block_rows, 0)
        d_block = lax.dynamic_slice_in_dim(d_heads, first_row, block_rows, 0)
        scores = (
            jnp.einsum("qhd,khd->hqk", q_block, key_rot, preferred_element_type=jnp.float32)
            * score_scale
        )
        masked = jnp.where(block_mask(first_row)[None], scores, -1e30)
        prob_rows = jnp.exp(masked - lse_block[..., None])
        d_probs = jnp.einsum("qhd,khd->hqk", d_block, values, preferred_element_type=jnp.float32)
        row_dot = jnp.sum(prob_rows * d_probs, axis=-1, keepdims=True)
        d_scores = (prob_rows * (d_probs - row_dot)).astype(jnp.bfloat16)
        d_query_block = (
            jnp.einsum("hqk,khd->qhd", d_scores, key_rot, preferred_element_type=jnp.float32)
            * score_scale
        )
        key_acc = (
            key_acc
            + jnp.einsum("hqk,qhd->khd", d_scores, q_block, preferred_element_type=jnp.float32)
            * score_scale
        )
        value_acc = value_acc + jnp.einsum(
            "hqk,qhd->khd",
            prob_rows.astype(jnp.bfloat16),
            d_block,
            preferred_element_type=jnp.float32,
        )
        return ((key_acc, value_acc), d_query_block)

    zero_grads = jnp.zeros((tree_len, local_heads, HD), jnp.float32)
    (d_key_rot, d_value_acc), d_query_blocks = lax.scan(
        attend_back, (zero_grads, zero_grads), (block_starts, lse_blocks)
    )
    d_query_rot = d_query_blocks.reshape(tree_len, local_heads, HD)
    d_qpre = (
        rotate_back(d_query_rot, cosine, sine_tab)
        .reshape(tree_len, local_heads * HD)
        .astype(jnp.bfloat16)
    )
    d_kpre = (
        rotate_back(d_key_rot, cosine, sine_tab)
        .reshape(tree_len, local_heads * HD)
        .astype(jnp.bfloat16)
    )
    d_value = d_value_acc.reshape(tree_len, local_heads * HD).astype(jnp.bfloat16)
    grad_query = inner_rows(normed_all, d_qpre)
    grad_key = inner_rows(normed_all, d_kpre)
    grad_value = inner_rows(normed_all, d_value)
    d_norm_one = lax.psum_scatter(
        (
            contract_last(d_qpre, w_query)
            + contract_last(d_kpre, w_key)
            + contract_last(d_value, w_value)
        ).astype(jnp.bfloat16),
        "mp",
        scatter_dimension=0,
        tiled=True,
    ).astype(jnp.float32)
    scaled_one = gain_attn * d_norm_one
    gain_attn_part = jnp.sum(d_norm_one * inputs_f32 * inv_one, axis=0)
    input_grad = (
        d_resid
        + inv_one * scaled_one
        - inputs_f32 * inv_one**3 * jnp.mean(scaled_one * inputs_f32, axis=-1, keepdims=True)
    )
    gain_attn_grad, gain_mlp_grad = lax.psum((gain_attn_part, gain_mlp_part), ("dp", "mp"))
    grad_query, grad_key, grad_value, grad_out, grad_gate, grad_up, grad_down = lax.psum(
        (grad_query, grad_key, grad_value, grad_out, grad_gate, grad_up, grad_down), "dp"
    )
    return (
        output,
        input_grad,
        gain_attn_grad,
        grad_query,
        grad_key,
        grad_value,
        grad_out,
        gain_mlp_grad,
        grad_gate,
        grad_up,
        grad_down,
    )


def solution(mesh):
    in_specs = (
        P(("dp", "mp"), None),
        P(),
        P(None, "mp"),
        P(None, "mp"),
        P(None, "mp"),
        P("mp", None),
        P(),
        P(None, "mp"),
        P(None, "mp"),
        P("mp", None),
        P("dp", None),
        P("dp", None),
        P(("dp", "mp"), None),
    )
    out_specs = (
        P(("dp", "mp"), None),
        P(("dp", "mp"), None),
        P(),
        P(None, "mp"),
        P(None, "mp"),
        P(None, "mp"),
        P("mp", None),
        P(),
        P(None, "mp"),
        P(None, "mp"),
        P("mp", None),
    )
    return jax.shard_map(
        on_device, mesh=mesh, in_specs=in_specs, out_specs=out_specs, check_vma=False
    )
```

profile of v0, /device:TPU:0, one launch (start us, length us, event | category | flops | bytes accessed | tf_op | source)
XLA Modules:
  0.0 983.7 jit_solution(3247048086694837235)
XLA Ops:
  16.7 35.2 %all-gather.5.cloned.1.call-done = bf16[1536,768]{1,0:T(8,128)(2,1)} async-done(((bf16[768,768]{1,0:T(8,128)(2,1)}), bf16[1536,768]{1,0:T(8,128)(2,1)}) %all-gather.5.cloned.1.call-update) | async-done | bytes 2359312 | tf_op jit(solution)/shard_map/all_gather | solution.py:109
  51.9 2.9 fusion.101
  60.2 82.6 %while.28 = (s32[]{:T(128)}, bf16[3,512,6,64]{1,3,2,0:T(8,128)(2,1)}, f32[3,6,512]{2,1,0:T(8,128)}, s32[3]{0:T(128)S(1)}, s32[1536,7]{0,1:T(8,128)}, /*index=5*/...) while((s32[]{:T(128)}, ...), condition=%wide.region_5.6_spmd.clone, body=%wide.region_2.5_spmd.clone.sunk | while | flops 1278167552 | bytes 63043776 | solution.py:133
  63.8 6.4 fusion.192
  70.2 4.8 fusion.193
  75.0 4.9 fusion.194
  79.9 7.5 fusion.195
  91.1 6.4 fusion.192
  97.5 4.8 fusion.193
  102.4 4.9 fusion.194
  107.2 7.5 fusion.195
  118.5 6.4 fusion.192
  124.8 4.8 fusion.193
  129.7 4.9 fusion.194
  134.5 7.5 fusion.195
  150.0 34.2 %reduce-scatter.5.cloned.1.call-done = bf16[768,768]{1,0:T(8,128)(2,1)} async-done(((bf16[1536,768]{1,0:T(8,128)(2,1)}), bf16[768,768]{1,0:T(8,128)(2,1)}) %reduce-scatter.5.cloned.1.call-update) | async-done | bytes 1179664 | tf_op jit(solution)/shard_map/reduce_scatter | solution.py:135
  188.7 35.6 %all-gather.7.cloned.1.call-done = bf16[1536,768]{1,0:T(8,128)(2,1)} async-done(((bf16[768,768]{1,0:T(8,128)(2,1)}), bf16[1536,768]{1,0:T(8,128)(2,1)}) %all-gather.7.cloned.1.call-update) | async-done | bytes 2359312 | tf_op jit(solution)/shard_map/all_gather | solution.py:144
  224.3 7.6 fusion.103
  231.9 4.4 fusion.102
  236.3 25.6 %all-gather.9.cloned.1.call-done = bf16[1536,768]{1,0:T(8,128)(2,1)} async-done(((bf16[768,768]{1,0:T(8,128)(2,1)}), bf16[1536,768]{1,0:T(8,128)(2,1)}) %all-gather.9.cloned.1.call-update) | async-done | bytes 2359312 | tf_op jit(solution)/shard_map/all_gather | solution.py:156
  261.9 10.2 %multiply_convert_fusion.1 = (bf16[1536,1024]{1,0:T(8,128)(2,1)S(1)}, bf16[1536,1024]{1,0:T(8,128)(2,1)S(1)}, bf16[1536,1024]{1,0:T(8,128)(2,1)}) fusion(f32[1536,1024]{1,0:T(8,128)} %fusion.102, f32[1536,1024]{1,0:T(8,128)} %fusion.103, bf16[1536,768]{1,0:T(8,128)(2,1)} %all-gather.9.cloned.1.call-done, bf16[1024,768]{1,0:T(8,128)(2,1)S(1)} %copy-done), kind=kOutput, calls=%fused_computation.61 | convolution fusion | flops 2439512064 | bytes 25952256 | tf_op jit(solution)/shard_map/dot_general | solution.py:61
  274.8 3.9 add_convert_fusion.1
  278.8 34.8 %reduce-scatter.9.cloned.1.call-done = bf16[768,768]{1,0:T(8,128)(2,1)} async-done(((bf16[1536,768]{1,0:T(8,128)(2,1)}), bf16[768,768]{1,0:T(8,128)(2,1)}) %reduce-scatter.9.cloned.1.call-update) | async-done | bytes 1179664 | tf_op jit(solution)/shard_map/reduce_scatter | solution.py:165
  313.7 3.8 fusion.64
  318.0 3.2 fusion.99
  321.3 36.2 %all-gather.11.cloned.1.call-done = bf16[1536,768]{1,0:T(8,128)(2,1)} async-done(((bf16[768,768]{1,0:T(8,128)(2,1)}), bf16[1536,768]{1,0:T(8,128)(2,1)}) %all-gather.11.cloned.1.call-update) | async-done | bytes 2359312 | tf_op jit(solution)/shard_map/all_gather | solution.py:178
  357.5 3.8 convolution_convert_fusion.2
  361.3 243.4 %while.29 = (s32[]{:T(128)}, f32[1536,6,64]{0,2,1:T(8,128)}, f32[1536,6,64]{0,2,1:T(8,128)}, f32[3,512,6,64]{1,0,3,2:T(4,128)}, s32[3]{0:T(128)S(1)}, /*index=5*...) while((s32[]{:T(128)}, f32[1536,6,64]{0,2,1:T(8,128)}, ...), condition=%wide.region_13.14_spmd.clone, body=%wide.region_11.13_spmd.clone.sunk | while | flops 3107211776 | bytes 262388048 | solution.py:216
  365.7 6.4 fusion.208
  372.1 3.8 fusion.207
  375.9 6.5 copy-done.1
  382.4 7.8 fusion.210
  390.2 14.7 %multiply_reduce_fusion.3 = (f32[6,512]{1,0:T(8,128)S(1)}, f32[6,512,1536]{2,1,0:T(8,128)}) fusion(f32[6,512,1536]{2,1,0:T(8,128)} %copy-done.1, f32[6,512]{1,0:T(8,128)S(1)} %dynamic-slice_bitcast_fusion.2, pred[512,1536]{1,0:T(8,128)(4,1)S(1)} %fusion.208, bf16[1536,6,64]{0,2,1:T(8,128)(2,1)S(1)} %copy-done.8, ...), kind=kOutput, calls=%fused_computation.28.clone.1 | convolution fusion | flops 627569664 | bytes 40132612 | tf_op jit(solution)/shard_map/while/body/eval_jaxpr/qhd,khd->hqk/dot_general | solution.py:195
  404.8 13.2 %multiply_convert_fusion.6 = bf16[6,512,1536]{2,1,0:T(8,128)(2,1)S(1)} fusion(f32[6,512,1536]{2,1,0:T(8,128)} %get-tuple-element.422, f32[6,512,1536]{2,1,0:T(8,128)} %copy-done.1, f32[6,512]{1,0:T(8,128)S(1)} %get-tuple-element.423, f32[6,512]{1,0:T(8,128)S(1)} %dynamic-slice_bitcast_fusion.2, pred[512,1536]{1,0:T(8,128)(4,1)S(1)} %fusion.208), kind=kLoop, calls=%fused_computation.27.clone.1 | loop fusion | flops 28311552 | bytes 47996928 | tf_op jit(solution)/shard_map/while/body/eval_jaxpr/convert_element_type | solution.py:197
  418.1 3.0 fusion.211
  421.1 3.0 fusion.209
  426.3 16.1 %dynamic_update_slice.22 = f32[3,512,6,64]{1,0,3,2:T(4,128)} dynamic-update-slice(f32[3,512,6,64]{1,0,3,2:T(4,128)} %get-tuple-element.478, f32[1,512,6,64]{1,0,3,2:T(1,128)S(1)} %copy.38, s32[]{:T(128)S(6)} %copy.55, s32[]{:T(128)} %constant.41.clone.1..sunk.1, s32[]{:T(128)} %constant.41.clone.1..sunk.1, s32[]{:T(128)} %constant.41.clone.1..sunk.1) | dynamic-update-slice | bytes 1572868 | tf_op jit(solution)/shard_map/while/body/jit(dynamic_update_index_in_dim)/dynamic_update_slice | solution.py:216
  446.5 6.4 fusion.208
  452.8 3.8 fusion.207
  456.6 6.5 copy-done.1
  463.1 8.2 fusion.210
  471.4 14.6 %multiply_reduce_fusion.3 = (f32[6,512]{1,0:T(8,128)S(1)}, f32[6,512,1536]{2,1,0:T(8,128)}) fusion(f32[6,512,1536]{2,1,0:T(8,128)} %copy-done.1, f32[6,512]{1,0:T(8,128)S(1)} %dynamic-slice_bitcast_fusion.2, pred[512,1536]{1,0:T(8,128)(4,1)S(1)} %fusion.208, bf16[1536,6,64]{0,2,1:T(8,128)(2,1)S(1)} %copy-done.8, ...), kind=kOutput, calls=%fused_computation.28.clone.1 | convolution fusion | flops 627569664 | bytes 40132612 | tf_op jit(solution)/shard_map/while/body/eval_jaxpr/qhd,khd->hqk/dot_general | solution.py:195
  486.0 13.2 %multiply_convert_fusion.6 = bf16[6,512,1536]{2,1,0:T(8,128)(2,1)S(1)} fusion(f32[6,512,1536]{2,1,0:T(8,128)} %get-tuple-element.422, f32[6,512,1536]{2,1,0:T(8,128)} %copy-done.1, f32[6,512]{1,0:T(8,128)S(1)} %get-tuple-element.423, f32[6,512]{1,0:T(8,128)S(1)} %dynamic-slice_bitcast_fusion.2, pred[512,1536]{1,0:T(8,128)(4,1)S(1)} %fusion.208), kind=kLoop, calls=%fused_computation.27.clone.1 | loop fusion | flops 28311552 | bytes 47996928 | tf_op jit(solution)/shard_map/while/body/eval_jaxpr/convert_element_type | solution.py:197
  499.2 3.0 fusion.211
  502.2 3.0 fusion.209
  507.5 16.1 %dynamic_update_slice.22 = f32[3,512,6,64]{1,0,3,2:T(4,128)} dynamic-update-slice(f32[3,512,6,64]{1,0,3,2:T(4,128)} %get-tuple-element.478, f32[1,512,6,64]{1,0,3,2:T(1,128)S(1)} %copy.38, s32[]{:T(128)S(6)} %copy.55, s32[]{:T(128)} %constant.41.clone.1..sunk.1, s32[]{:T(128)} %constant.41.clone.1..sunk.1, s32[]{:T(128)} %constant.41.clone.1..sunk.1) | dynamic-update-slice | bytes 1572868 | tf_op jit(solution)/shard_map/while/body/jit(dynamic_update_index_in_dim)/dynamic_update_slice | solution.py:216
  527.6 6.4 fusion.208
  533.9 3.7 fusion.207
  537.7 6.5 copy-done.1
  544.2 8.2 fusion.210
  552.4 14.6 %multiply_reduce_fusion.3 = (f32[6,512]{1,0:T(8,128)S(1)}, f32[6,512,1536]{2,1,0:T(8,128)}) fusion(f32[6,512,1536]{2,1,0:T(8,128)} %copy-done.1, f32[6,512]{1,0:T(8,128)S(1)} %dynamic-slice_bitcast_fusion.2, pred[512,1536]{1,0:T(8,128)(4,1)S(1)} %fusion.208, bf16[1536,6,64]{0,2,1:T(8,128)(2,1)S(1)} %copy-done.8, ...), kind=kOutput, calls=%fused_computation.28.clone.1 | convolution fusion | flops 627569664 | bytes 40132612 | tf_op jit(solution)/shard_map/while/body/eval_jaxpr/qhd,khd->hqk/dot_general | solution.py:195
  567.0 13.2 %multiply_convert_fusion.6 = bf16[6,512,1536]{2,1,0:T(8,128)(2,1)S(1)} fusion(f32[6,512,1536]{2,1,0:T(8,128)} %get-tuple-element.422, f32[6,512,1536]{2,1,0:T(8,128)} %copy-done.1, f32[6,512]{1,0:T(8,128)S(1)} %get-tuple-element.423, f32[6,512]{1,0:T(8,128)S(1)} %dynamic-slice_bitcast_fusion.2, pred[512,1536]{1,0:T(8,128)(4,1)S(1)} %fusion.208), kind=kLoop, calls=%fused_computation.27.clone.1 | loop fusion | flops 28311552 | bytes 47996928 | tf_op jit(solution)/shard_map/while/body/eval_jaxpr/convert_element_type | solution.py:197
  580.2 3.0 fusion.211
  583.2 3.0 fusion.209
  588.4 16.1 %dynamic_update_slice.22 = f32[3,512,6,64]{1,0,3,2:T(4,128)} dynamic-update-slice(f32[3,512,6,64]{1,0,3,2:T(4,128)} %get-tuple-element.478, f32[1,512,6,64]{1,0,3,2:T(1,128)S(1)} %copy.38, s32[]{:T(128)S(6)} %copy.55, s32[]{:T(128)} %constant.41.clone.1..sunk.1, s32[]{:T(128)} %constant.41.clone.1..sunk.1, s32[]{:T(128)} %constant.41.clone.1..sunk.1) | dynamic-update-slice | bytes 1572868 | tf_op jit(solution)/shard_map/while/body/jit(dynamic_update_index_in_dim)/dynamic_update_slice | solution.py:216
  604.6 4.9 reshape.176
  622.3 5.9 convolution_convert_fusion
  628.6 7.2 fusion.113
  635.8 4.4 fusion.112
  640.2 4.4 fusion.111
  654.1 3.1 reduce-scatter.11.cloned.1.call-done
  659.5 39.7 %all-reduce = (f32[768]{0:T(1024)}, f32[768]{0:T(1024)}) all-reduce(f32[768]{0:T(1024)S(1)} %get-tuple-element.206, f32[768]{0:T(1024)S(1)} %copy-done.47), channel_id=1, replica_groups=mesh['dp'=16,'mp'=2] {'dp','mp'}, use_global_device_ids=true, to_apply=%region_17.18 | all-reduce | flops 1536 | bytes 12288 | tf_op jit(solution)/shard_map/psum | solution.py:251
  699.3 5.1 fusion.59
  704.4 258.5 %all-reduce.4.cloned.1.call-done = (f32[768,384]{1,0:T(8,128)}, f32[768,384]{1,0:T(8,128)}, f32[768,384]{1,0:T(8,128)}, f32[384,768]{1,0:T(8,128)}, f32[768,1024...) async-done(((f32[768,384]{1,0:T(8,128)}, f32[768,384]{1,0:T(8,128)}, f32[768,384]{1,0:T(8,128)}, f32[384,768]{1,0:T(8,128)}, f32[768,1024]{1,0:T(8,128)}, ...) | async-done | bytes 14155792 | tf_op jit(solution)/shard_map/psum | solution.py:252
  (233 shorter events, 86.9 us)
Async XLA Ops:
  7.2 254.7 %copy-start = (bf16[1024,768]{1,0:T(8,128)(2,1)S(1)}, bf16[1024,768]{1,0:T(8,128)(2,1)}, u32[]{:S(2)}) copy-start(bf16[1024,768]{1,0:T(8,128)(2,1)} %param.26) | copy-start | bytes 4718596
  7.2 44.7 %all-gather.5.cloned.1.call-start = ((), (), s32[]{:S(2)}) async-start(), calls=%async_computation.4 | async-start | bytes 3538944 | tf_op jit(solution)/shard_map/all_gather | solution.py:109
  8.0 4.9 copy-start.40
  8.0 5.0 copy-start.59
  8.0 5.9 copy-start.58
  10.2 4.6 copy-start.38
  10.2 41.6 %copy-start.30 = (bf16[768,384]{1,0:T(8,128)(2,1)S(1)}, bf16[768,384]{1,0:T(8,128)(2,1)}, u32[]{:S(2)}) copy-start(bf16[768,384]{1,0:T(8,128)(2,1)} %param.20) | copy-start | bytes 1769476
  13.0 171.3 %reduce-scatter.5.cloned.1.call-start = ((), (), s32[]{:S(2)}) async-start(), calls=%async_computation.5 | async-start | bytes 3538944 | tf_op jit(solution)/shard_map/reduce_scatter | solution.py:135
  16.7 39.3 %copy-start.19 = (f32[1536,32]{0,1:T(8,128)}, f32[1536,32]{0,1:T(8,128)S(1)}, u32[]{:S(2)}) copy-start(f32[1536,32]{0,1:T(8,128)S(1)} %get-tuple-element.280) | copy-start | bytes 589828
  16.7 39.3 %copy-start.21 = (f32[1536,32]{0,1:T(8,128)}, f32[1536,32]{0,1:T(8,128)S(1)}, u32[]{:S(2)}) copy-start(f32[1536,32]{0,1:T(8,128)S(1)} %get-tuple-element.281) | copy-start | bytes 589828
  16.7 38.1 %copy-start.28 = (bf16[768,384]{1,0:T(8,128)(2,1)S(1)}, bf16[768,384]{1,0:T(8,128)(2,1)}, u32[]{:S(2)}) copy-start(bf16[768,384]{1,0:T(8,128)(2,1)} %param.19) | copy-start | bytes 1769476
  51.9 3.0 copy-start.49
  142.8 3.7 copy-start.57
  149.4 74.9 %all-gather.7.cloned.1.call-start = ((), (), s32[]{:S(2)}) async-start(), calls=%async_computation.6 | async-start | bytes 3538944 | tf_op jit(solution)/shard_map/all_gather | solution.py:144
  150.0 167.4 %copy-start.34 = (f32[768]{0:T(1024)}, f32[768]{0:T(1024)S(1)}, u32[]{:S(2)}) copy-start(f32[768]{0:T(1024)S(1)} %convert_element_type.122) | copy-start | bytes 9220
  186.5 130.9 %copy-start.36 = (f32[768]{0:T(1024)}, f32[768]{0:T(1024)S(1)}, u32[]{:S(2)}) copy-start(f32[768]{0:T(1024)S(1)} %get-tuple-element.285) | copy-start | bytes 9220
  186.5 130.9 %copy-start.42 = (f32[768]{0:T(1024)}, f32[768]{0:T(1024)S(1)}, u32[]{:S(2)}) copy-start(f32[768]{0:T(1024)S(1)} %get-tuple-element.284) | copy-start | bytes 9220
  188.1 73.8 %all-gather.9.cloned.1.call-start = ((), (), s32[]{:S(2)}) async-start(), calls=%async_computation.8 | async-start | bytes 3538944 | tf_op jit(solution)/shard_map/all_gather | solution.py:156
  188.6 125.0 %reduce-scatter.9.cloned.1.call-start = ((), (), s32[]{:S(2)}) async-start(), calls=%async_computation.9 | async-start | bytes 3538944 | tf_op jit(solution)/shard_map/reduce_scatter | solution.py:165
  224.3 7.6 copy-start.51
  224.3 7.6 copy-start.54
  261.9 10.2 %copy-start.55 = (bf16[768,1024]{1,0:T(8,128)(2,1)S(1)}, bf16[768,1024]{1,0:T(8,128)(2,1)}, u32[]{:S(2)}) copy-start(bf16[768,1024]{1,0:T(8,128)(2,1)} %param.24) | copy-start | bytes 4718596
  272.1 2.7 copy-start.60
  272.1 2.7 copy-start.62
  272.1 2.7 copy-start.56
  278.8 78.7 %all-gather.11.cloned.1.call-start = ((), (), s32[]{:S(2)}) async-start(), calls=%async_computation.10 | async-start | bytes 3538944 | tf_op jit(solution)/shard_map/all_gather | solution.py:178
  313.7 4.4 copy-start.6
  313.7 4.4 copy-start.10
  313.7 4.4 copy-start.11
  321.2 335.9 %reduce-scatter.11.cloned.1.call-start = ((), (), s32[]{:S(2)}) async-start(), calls=%async_computation.11 | async-start | bytes 3538944 | tf_op jit(solution)/shard_map/reduce_scatter | solution.py:234
  375.9 6.5 copy-start.1
  382.4 7.8 copy-start.8
  418.1 3.0 copy-start.2
  456.6 6.5 copy-start.1
  463.1 8.3 copy-start.8
  499.2 3.0 copy-start.2
  537.7 6.5 copy-start.1
  544.2 8.2 copy-start.8
  580.2 3.0 copy-start.2
  609.5 2.4 copy-start.22
  611.5 7.9 copy-start.14
  616.9 2.5 copy-start.12
  622.3 77.0 %reduce-scatter.7.cloned.1.call-start = ((), (), s32[]{:S(2)}) async-start(), calls=%async_computation.7 | async-start | bytes 3538944 | tf_op jit(solution)/shard_map/reduce_scatter | solution.py:150
  628.3 334.6 %all-reduce.4.cloned.1.call-start = ((), (), s32[]{:S(2)}) async-start(), calls=%async_computation.12 | async-start | bytes 28311552 | tf_op jit(solution)/shard_map/psum | solution.py:252
  628.5 7.2 copy-start.52
  628.5 7.2 copy-start.63
  635.8 4.4 copy-start.61
  640.2 4.4 copy-start.27
  640.2 4.4 copy-start.53
  649.1 2.4 copy-start.15
  654.0 3.2 copy-start.7
  654.0 3.2 copy-start.39
  654.0 3.2 copy-start.41
  654.0 5.5 copy-start.47
  654.0 45.3 %copy-start.35 = (f32[768]{0:T(1024)S(1)}, f32[768]{0:T(1024)}, u32[]{:S(2)}) copy-start(f32[768]{0:T(1024)} %copy-done.34) | copy-start | bytes 9220
  654.0 45.3 %copy-start.37 = (f32[768]{0:T(1024)S(1)}, f32[768]{0:T(1024)}, u32[]{:S(2)}) copy-start(f32[768]{0:T(1024)} %copy-done.36) | copy-start | bytes 9220
  654.0 45.3 %copy-start.43 = (f32[768]{0:T(1024)S(1)}, f32[768]{0:T(1024)}, u32[]{:S(2)}) copy-start(f32[768]{0:T(1024)} %copy-done.42) | copy-start | bytes 9220
  654.1 45.3 %copy-start.45 = (f32[768]{0:T(1024)S(1)}, f32[768]{0:T(1024)}, u32[]{:S(2)}) copy-start(f32[768]{0:T(1024)} %copy-done.44) | copy-start | bytes 9220
  654.1 45.3 %copy-start.46 = (f32[768]{0:T(1024)S(1)}, f32[768]{0:T(1024)}, u32[]{:S(2)}) copy-start(f32[768]{0:T(1024)} %get-tuple-element.282) | copy-start | bytes 9220
  962.9 2.5 copy-start.25
  962.9 3.5 copy-start.24
  966.4 2.8 copy-start.18
  969.2 3.0 copy-start.17
  972.2 3.0 copy-start.16
  (17 other events, 27.1 us)
Sparse Core Ops, SparseCore 0:
  13.1 38.7 all-gather.4
  149.5 34.7 reduce-scatter.4
  188.2 36.0 all-gather.6
  225.8 36.0 all-gather.8
  278.9 34.6 reduce-scatter.8
  321.4 36.0 all-gather.10
  622.4 34.7 reduce-scatter.10
  660.1 35.1 reduce-scatter.6
  701.8 260.9 all-reduce.3
where the time goes:
time: 992 us; the launch traced here: 984 us
  waiting for transfers between devices  464 us (47%)
  matrix products  254 us (26%)
  local copies, waits for them, and re-layouts  107 us (11%)
  other arithmetic  91.1 us (9%)
  blocking collectives  39.7 us (4%)
  between operations  14.7 us (1%)
  loops' own time  13.4 us (1%)
    psum x1, waiting for transfers between devices, on_device(): lax.psum((grad_query, grad_key, grad_value, grad_out, grad_gate, grad_up,...  258 us
    dynamic_update_slice x6, local copies, waits for them, and re-layouts, on_device(): lax.scan(attend_back, (zero_grads, zero_grads), (block_starts, lse_blocks))  50.6 us
    dot_general x3, matrix products, attend_back(): jnp.einsum('qhd,khd->hqk', d_block, values, preferred_element_type=jnp.fl...  43.8 us
    psum x1, blocking collectives, on_device(): lax.psum((gain_attn_part, gain_mlp_part), ('dp', 'mp'))  39.7 us
    convert_element_type x3, other arithmetic, attend_back(): d_scores = (prob_rows * (d_probs - row_dot)).astype(jnp.bfloat16)  39.7 us
    dot_general x6, matrix products, block_mask(): jnp.dot(vis_block, onehot.T) > 0  38.2 us
    all_gather x1, waiting for transfers between devices, on_device(): lax.all_gather(d_resid.astype(jnp.bfloat16), 'mp', axis=0, tiled=True)  36.2 us
    all_gather x1, waiting for transfers between devices, on_device(): normed_two_all = lax.all_gather(normed_two, 'mp', axis=0, tiled=True)  35.6 us
  transfers between devices with their start and end apart: 9, of which 8 were waited for; matrix products, arithmetic and copies ran while one was open for 6% of the time, Pallas kernels for 0%

commit v1 on v0

--- a/solution.py
+++ b/solution.py
@@ -248,7 +248,7 @@
         + inv_one * scaled_one
         - inputs_f32 * inv_one**3 * jnp.mean(scaled_one * inputs_f32, axis=-1, keepdims=True)
     )
-    gain_attn_grad, gain_mlp_grad = lax.psum((gain_attn_part, gain_mlp_part), ("dp", "mp"))
+    gain_attn_grad, gain_mlp_grad = lax.psum(lax.psum((gain_attn_part, gain_mlp_part), "dp"), "mp")
     grad_query, grad_key, grad_value, grad_out, grad_gate, grad_up, grad_down = lax.psum(
         (grad_query, grad_key, grad_value, grad_out, grad_gate, grad_up, grad_down), "dp"
     )

time: 992 us -> 992 us (level)
    psum x1 -> x2, blocking collectives: 39.7 us -> 39.3 us  [the longest x1 33.7 us: on_device(): lax.psum((gain_attn_part, gain_mlp_part), 'dp')]
    while x24 -> x18, local copies, waits for them, and re-layouts: 23.6 us -> 23.6 us
where the time goes in v1:
time: 992 us; the launch traced here: 983 us
  waiting for transfers between devices  464 us (47%)
  matrix products  254 us (26%)
  local copies, waits for them, and re-layouts  107 us (11%)
  other arithmetic  91 us (9%)
  blocking collectives  39.3 us (4%)
  between operations  14.7 us (1%)
  loops' own time  13 us (1%)
    psum x1, waiting for transfers between devices, on_device(): lax.psum((grad_query, grad_key, grad_value, grad_out, grad_gate, grad_up,...  259 us
    dynamic_update_slice x6, local copies, waits for them, and re-layouts, on_device(): lax.scan(attend_back, (zero_grads, zero_grads), (block_starts, lse_blocks))  50.6 us
    dot_general x3, matrix products, attend_back(): jnp.einsum('qhd,khd->hqk', d_block, values, preferred_element_type=jnp.fl...  44.1 us
    convert_element_type x3, other arithmetic, attend_back(): d_scores = (prob_rows * (d_probs - row_dot)).astype(jnp.bfloat16)  39.7 us
    dot_general x6, matrix products, block_mask(): jnp.dot(vis_block, onehot.T) > 0  38.2 us
    all_gather x1, waiting for transfers between devices, on_device(): lax.all_gather(d_resid.astype(jnp.bfloat16), 'mp', axis=0, tiled=True)  36.2 us
    all_gather x1, waiting for transfers between devices, on_device(): normed_two_all = lax.all_gather(normed_two, 'mp', axis=0, tiled=True)  35.6 us
    all_gather x1, waiting for transfers between devices, on_device(): normed_all = lax.all_gather(normed, 'mp', axis=0, tiled=True)  35.2 us
  transfers between devices with their start and end apart: 9, of which 8 were waited for; matrix products, arithmetic and copies ran while one was open for 6% of the time, Pallas kernels for 0%

profile of v1, /device:TPU:0, one launch (start us, length us, event | category | flops | bytes accessed | tf_op | source)
XLA Modules:
  0.0 983.4 jit_solution(17907645116783695451)
XLA Ops:
  17.3 35.2 %all-gather.5.cloned.1.call-done = bf16[1536,768]{1,0:T(8,128)(2,1)} async-done(((bf16[768,768]{1,0:T(8,128)(2,1)}), bf16[1536,768]{1,0:T(8,128)(2,1)}) %all-gather.5.cloned.1.call-update) | async-done | bytes 2359312 | tf_op jit(solution)/shard_map/all_gather | solution.py:109
  60.7 82.6 %while.28 = (s32[]{:T(128)}, bf16[3,512,6,64]{1,3,2,0:T(8,128)(2,1)}, f32[3,6,512]{2,1,0:T(8,128)}, s32[3]{0:T(128)S(1)}, s32[1536,7]{0,1:T(8,128)}, /*index=5*/...) while((s32[]{:T(128)}, ...), condition=%wide.region_5.6_spmd.clone, body=%wide.region_2.5_spmd.clone.sunk | while | flops 1278167552 | bytes 63043776 | solution.py:133
  64.4 6.4 fusion.192
  70.7 4.8 fusion.193
  75.6 4.9 fusion.194
  80.4 7.5 fusion.195
  91.7 6.4 fusion.192
  98.1 4.8 fusion.193
  102.9 4.9 fusion.194
  107.8 7.5 fusion.195
  119.0 6.4 fusion.192
  125.4 4.8 fusion.193
  130.2 4.9 fusion.194
  135.1 7.5 fusion.195
  150.6 34.2 %reduce-scatter.5.cloned.1.call-done = bf16[768,768]{1,0:T(8,128)(2,1)} async-done(((bf16[1536,768]{1,0:T(8,128)(2,1)}), bf16[768,768]{1,0:T(8,128)(2,1)}) %reduce-scatter.5.cloned.1.call-update) | async-done | bytes 1179664 | tf_op jit(solution)/shard_map/reduce_scatter | solution.py:135
  189.3 35.6 %all-gather.7.cloned.1.call-done = bf16[1536,768]{1,0:T(8,128)(2,1)} async-done(((bf16[768,768]{1,0:T(8,128)(2,1)}), bf16[1536,768]{1,0:T(8,128)(2,1)}) %all-gather.7.cloned.1.call-update) | async-done | bytes 2359312 | tf_op jit(solution)/shard_map/all_gather | solution.py:144
  224.9 7.6 fusion.103
  232.5 4.5 fusion.102
  236.9 25.5 %all-gather.9.cloned.1.call-done = bf16[1536,768]{1,0:T(8,128)(2,1)} async-done(((bf16[768,768]{1,0:T(8,128)(2,1)}), bf16[1536,768]{1,0:T(8,128)(2,1)}) %all-gather.9.cloned.1.call-update) | async-done | bytes 2359312 | tf_op jit(solution)/shard_map/all_gather | solution.py:156
  262.5 10.2 %multiply_convert_fusion.1 = (bf16[1536,1024]{1,0:T(8,128)(2,1)S(1)}, bf16[1536,1024]{1,0:T(8,128)(2,1)S(1)}, bf16[1536,1024]{1,0:T(8,128)(2,1)}) fusion(f32[1536,1024]{1,0:T(8,128)} %fusion.102, f32[1536,1024]{1,0:T(8,128)} %fusion.103, bf16[1536,768]{1,0:T(8,128)(2,1)} %all-gather.9.cloned.1.call-done, bf16[1024,768]{1,0:T(8,128)(2,1)S(1)} %copy-done), kind=kOutput, calls=%fused_computation.61 | convolution fusion | flops 2439512064 | bytes 25952256 | tf_op jit(solution)/shard_map/dot_general | solution.py:61
  275.4 3.9 add_convert_fusion.1
  279.4 34.8 %reduce-scatter.9.cloned.1.call-done = bf16[768,768]{1,0:T(8,128)(2,1)} async-done(((bf16[1536,768]{1,0:T(8,128)(2,1)}), bf16[768,768]{1,0:T(8,128)(2,1)}) %reduce-scatter.9.cloned.1.call-update) | async-done | bytes 1179664 | tf_op jit(solution)/shard_map/reduce_scatter | solution.py:165
  314.2 3.8 fusion.64
  318.6 3.2 fusion.99
  321.9 36.2 %all-gather.11.cloned.1.call-done = bf16[1536,768]{1,0:T(8,128)(2,1)} async-done(((bf16[768,768]{1,0:T(8,128)(2,1)}), bf16[1536,768]{1,0:T(8,128)(2,1)}) %all-gather.11.cloned.1.call-update) | async-done | bytes 2359312 | tf_op jit(solution)/shard_map/all_gather | solution.py:178
  358.0 3.8 convolution_convert_fusion.2
  361.8 242.9 %while.29 = (s32[]{:T(128)}, f32[1536,6,64]{0,2,1:T(8,128)}, f32[1536,6,64]{0,2,1:T(8,128)}, f32[3,512,6,64]{1,0,3,2:T(4,128)}, s32[3]{0:T(128)S(1)}, /*index=5*...) while((s32[]{:T(128)}, f32[1536,6,64]{0,2,1:T(8,128)}, ...), condition=%wide.region_13.14_spmd.clone, body=%wide.region_11.13_spmd.clone.sunk | while | flops 3107211776 | bytes 257669424 | solution.py:216
  366.1 6.4 fusion.208
  372.5 3.8 fusion.207
  376.3 6.5 copy-done.1
  382.8 7.7 fusion.210
  390.5 14.7 %multiply_reduce_fusion.3 = (f32[6,512]{1,0:T(8,128)S(1)}, f32[6,512,1536]{2,1,0:T(8,128)}) fusion(f32[6,512,1536]{2,1,0:T(8,128)} %copy-done.1, f32[6,512]{1,0:T(8,128)S(1)} %dynamic-slice_bitcast_fusion.2, pred[512,1536]{1,0:T(8,128)(4,1)S(1)} %fusion.208, bf16[1536,6,64]{0,2,1:T(8,128)(2,1)} %get-tuple-element.502, ...), kind=kOutput, calls=%fused_computation.28.clone.1 | convolution fusion | flops 627569664 | bytes 40132612 | tf_op jit(solution)/shard_map/while/body/eval_jaxpr/qhd,khd->hqk/dot_general | solution.py:195
  405.2 13.2 %multiply_convert_fusion.6 = bf16[6,512,1536]{2,1,0:T(8,128)(2,1)S(1)} fusion(f32[6,512,1536]{2,1,0:T(8,128)} %get-tuple-element.424, f32[6,512,1536]{2,1,0:T(8,128)} %copy-done.1, f32[6,512]{1,0:T(8,128)S(1)} %get-tuple-element.425, f32[6,512]{1,0:T(8,128)S(1)} %dynamic-slice_bitcast_fusion.2, pred[512,1536]{1,0:T(8,128)(4,1)S(1)} %fusion.208), kind=kLoop, calls=%fused_computation.27.clone.1 | loop fusion | flops 28311552 | bytes 47996928 | tf_op jit(solution)/shard_map/while/body/eval_jaxpr/convert_element_type | solution.py:197
  418.5 3.0 fusion.211
  421.4 3.0 fusion.209
  426.7 16.1 %dynamic_update_slice.22 = f32[3,512,6,64]{1,0,3,2:T(4,128)} dynamic-update-slice(f32[3,512,6,64]{1,0,3,2:T(4,128)} %get-tuple-element.480, f32[1,512,6,64]{1,0,3,2:T(1,128)S(1)} %copy.38, s32[]{:T(128)S(6)} %copy.55, s32[]{:T(128)} %constant.41.clone.1..sunk.1, s32[]{:T(128)} %constant.41.clone.1..sunk.1, s32[]{:T(128)} %constant.41.clone.1..sunk.1) | dynamic-update-slice | bytes 1572868 | tf_op jit(solution)/shard_map/while/body/jit(dynamic_update_index_in_dim)/dynamic_update_slice | solution.py:216
  446.6 6.4 fusion.208
  453.0 3.8 fusion.207
  456.8 6.5 copy-done.1
  463.3 8.2 fusion.210
  471.5 14.7 %multiply_reduce_fusion.3 = (f32[6,512]{1,0:T(8,128)S(1)}, f32[6,512,1536]{2,1,0:T(8,128)}) fusion(f32[6,512,1536]{2,1,0:T(8,128)} %copy-done.1, f32[6,512]{1,0:T(8,128)S(1)} %dynamic-slice_bitcast_fusion.2, pred[512,1536]{1,0:T(8,128)(4,1)S(1)} %fusion.208, bf16[1536,6,64]{0,2,1:T(8,128)(2,1)} %get-tuple-element.502, ...), kind=kOutput, calls=%fused_computation.28.clone.1 | convolution fusion | flops 627569664 | bytes 40132612 | tf_op jit(solution)/shard_map/while/body/eval_jaxpr/qhd,khd->hqk/dot_general | solution.py:195
  486.1 13.2 %multiply_convert_fusion.6 = bf16[6,512,1536]{2,1,0:T(8,128)(2,1)S(1)} fusion(f32[6,512,1536]{2,1,0:T(8,128)} %get-tuple-element.424, f32[6,512,1536]{2,1,0:T(8,128)} %copy-done.1, f32[6,512]{1,0:T(8,128)S(1)} %get-tuple-element.425, f32[6,512]{1,0:T(8,128)S(1)} %dynamic-slice_bitcast_fusion.2, pred[512,1536]{1,0:T(8,128)(4,1)S(1)} %fusion.208), kind=kLoop, calls=%fused_computation.27.clone.1 | loop fusion | flops 28311552 | bytes 47996928 | tf_op jit(solution)/shard_map/while/body/eval_jaxpr/convert_element_type | solution.py:197
  499.4 3.0 fusion.211
  502.4 3.0 fusion.209
  507.6 16.1 %dynamic_update_slice.22 = f32[3,512,6,64]{1,0,3,2:T(4,128)} dynamic-update-slice(f32[3,512,6,64]{1,0,3,2:T(4,128)} %get-tuple-element.480, f32[1,512,6,64]{1,0,3,2:T(1,128)S(1)} %copy.38, s32[]{:T(128)S(6)} %copy.55, s32[]{:T(128)} %constant.41.clone.1..sunk.1, s32[]{:T(128)} %constant.41.clone.1..sunk.1, s32[]{:T(128)} %constant.41.clone.1..sunk.1) | dynamic-update-slice | bytes 1572868 | tf_op jit(solution)/shard_map/while/body/jit(dynamic_update_index_in_dim)/dynamic_update_slice | solution.py:216
  527.6 6.4 fusion.208
  533.9 3.7 fusion.207
  537.7 6.5 copy-done.1
  544.2 8.2 fusion.210
  552.3 14.7 %multiply_reduce_fusion.3 = (f32[6,512]{1,0:T(8,128)S(1)}, f32[6,512,1536]{2,1,0:T(8,128)}) fusion(f32[6,512,1536]{2,1,0:T(8,128)} %copy-done.1, f32[6,512]{1,0:T(8,128)S(1)} %dynamic-slice_bitcast_fusion.2, pred[512,1536]{1,0:T(8,128)(4,1)S(1)} %fusion.208, bf16[1536,6,64]{0,2,1:T(8,128)(2,1)} %get-tuple-element.502, ...), kind=kOutput, calls=%fused_computation.28.clone.1 | convolution fusion | flops 627569664 | bytes 40132612 | tf_op jit(solution)/shard_map/while/body/eval_jaxpr/qhd,khd->hqk/dot_general | solution.py:195
  567.0 13.2 %multiply_convert_fusion.6 = bf16[6,512,1536]{2,1,0:T(8,128)(2,1)S(1)} fusion(f32[6,512,1536]{2,1,0:T(8,128)} %get-tuple-element.424, f32[6,512,1536]{2,1,0:T(8,128)} %copy-done.1, f32[6,512]{1,0:T(8,128)S(1)} %get-tuple-element.425, f32[6,512]{1,0:T(8,128)S(1)} %dynamic-slice_bitcast_fusion.2, pred[512,1536]{1,0:T(8,128)(4,1)S(1)} %fusion.208), kind=kLoop, calls=%fused_computation.27.clone.1 | loop fusion | flops 28311552 | bytes 47996928 | tf_op jit(solution)/shard_map/while/body/eval_jaxpr/convert_element_type | solution.py:197
  580.3 3.0 fusion.211
  583.3 3.0 fusion.209
  588.5 16.1 %dynamic_update_slice.22 = f32[3,512,6,64]{1,0,3,2:T(4,128)} dynamic-update-slice(f32[3,512,6,64]{1,0,3,2:T(4,128)} %get-tuple-element.480, f32[1,512,6,64]{1,0,3,2:T(1,128)S(1)} %copy.38, s32[]{:T(128)S(6)} %copy.55, s32[]{:T(128)} %constant.41.clone.1..sunk.1, s32[]{:T(128)} %constant.41.clone.1..sunk.1, s32[]{:T(128)} %constant.41.clone.1..sunk.1) | dynamic-update-slice | bytes 1572868 | tf_op jit(solution)/shard_map/while/body/jit(dynamic_update_index_in_dim)/dynamic_update_slice | solution.py:216
  604.7 4.8 reshape.176
  622.4 5.9 convolution_convert_fusion
  628.6 7.2 fusion.113
  635.8 4.4 fusion.112
  640.2 4.4 fusion.111
  654.1 3.1 reduce-scatter.11.cloned.1.call-done
  659.6 33.7 %all-reduce = (f32[768]{0:T(1024)S(1)}, f32[768]{0:T(1024)S(1)}) all-reduce(f32[768]{0:T(1024)S(1)} %get-tuple-element.206, f32[768]{0:T(1024)S(1)} %copy-done.46), channel_id=1, replica_groups=mesh['dp'=16,'mp'=2] {'dp'}, use_global_device_ids=true, to_apply=%region_17.18 | all-reduce | flops 1536 | bytes 12288 | tf_op jit(solution)/shard_map/psum | solution.py:251
  693.3 5.6 all-reduce.2
  698.9 5.1 fusion.59
  704.0 258.6 %all-reduce.5.cloned.1.call-done = (f32[768,384]{1,0:T(8,128)}, f32[768,384]{1,0:T(8,128)}, f32[768,384]{1,0:T(8,128)}, f32[384,768]{1,0:T(8,128)}, f32[768,1024...) async-done(((f32[768,384]{1,0:T(8,128)}, f32[768,384]{1,0:T(8,128)}, f32[768,384]{1,0:T(8,128)}, f32[384,768]{1,0:T(8,128)}, f32[768,1024]{1,0:T(8,128)}, ...) | async-done | bytes 14155792 | tf_op jit(solution)/shard_map/psum | solution.py:252
  (228 shorter events, 90.2 us)
Async XLA Ops:
  7.2 255.3 %copy-start = (bf16[1024,768]{1,0:T(8,128)(2,1)S(1)}, bf16[1024,768]{1,0:T(8,128)(2,1)}, u32[]{:S(2)}) copy-start(bf16[1024,768]{1,0:T(8,128)(2,1)} %param.26) | copy-start | bytes 4718596
  7.2 45.3 %all-gather.5.cloned.1.call-start = ((), (), s32[]{:S(2)}) async-start(), calls=%async_computation.4 | async-start | bytes 3538944 | tf_op jit(solution)/shard_map/all_gather | solution.py:109
  8.0 2.2 copy-start.39
  8.0 5.6 copy-start.58
  8.0 6.5 copy-start.57
  10.8 41.6 %copy-start.29 = (bf16[768,384]{1,0:T(8,128)(2,1)S(1)}, bf16[768,384]{1,0:T(8,128)(2,1)}, u32[]{:S(2)}) copy-start(bf16[768,384]{1,0:T(8,128)(2,1)} %param.20) | copy-start | bytes 1769476
  13.5 171.3 %reduce-scatter.5.cloned.1.call-start = ((), (), s32[]{:S(2)}) async-start(), calls=%async_computation.5 | async-start | bytes 3538944 | tf_op jit(solution)/shard_map/reduce_scatter | solution.py:135
  17.2 39.3 %copy-start.18 = (f32[1536,32]{0,1:T(8,128)}, f32[1536,32]{0,1:T(8,128)S(1)}, u32[]{:S(2)}) copy-start(f32[1536,32]{0,1:T(8,128)S(1)} %get-tuple-element.282) | copy-start | bytes 589828
  17.3 39.3 %copy-start.20 = (f32[1536,32]{0,1:T(8,128)}, f32[1536,32]{0,1:T(8,128)S(1)}, u32[]{:S(2)}) copy-start(f32[1536,32]{0,1:T(8,128)S(1)} %get-tuple-element.283) | copy-start | bytes 589828
  17.3 38.1 %copy-start.27 = (bf16[768,384]{1,0:T(8,128)(2,1)S(1)}, bf16[768,384]{1,0:T(8,128)(2,1)}, u32[]{:S(2)}) copy-start(bf16[768,384]{1,0:T(8,128)(2,1)} %param.19) | copy-start | bytes 1769476
  52.5 3.0 copy-start.48
  143.3 3.7 copy-start.56
  149.9 74.9 %all-gather.7.cloned.1.call-start = ((), (), s32[]{:S(2)}) async-start(), calls=%async_computation.6 | async-start | bytes 3538944 | tf_op jit(solution)/shard_map/all_gather | solution.py:144
  150.6 167.4 %copy-start.33 = (f32[768]{0:T(1024)}, f32[768]{0:T(1024)S(1)}, u32[]{:S(2)}) copy-start(f32[768]{0:T(1024)S(1)} %convert_element_type.122) | copy-start | bytes 9220
  184.8 2.3 copy-start.5
  184.8 2.3 copy-start.8
  187.1 131.0 %copy-start.35 = (f32[768]{0:T(1024)}, f32[768]{0:T(1024)S(1)}, u32[]{:S(2)}) copy-start(f32[768]{0:T(1024)S(1)} %get-tuple-element.287) | copy-start | bytes 9220
  187.1 130.9 %copy-start.41 = (f32[768]{0:T(1024)}, f32[768]{0:T(1024)S(1)}, u32[]{:S(2)}) copy-start(f32[768]{0:T(1024)S(1)} %get-tuple-element.286) | copy-start | bytes 9220
  188.6 73.8 %all-gather.9.cloned.1.call-start = ((), (), s32[]{:S(2)}) async-start(), calls=%async_computation.8 | async-start | bytes 3538944 | tf_op jit(solution)/shard_map/all_gather | solution.py:156
  189.2 125.0 %reduce-scatter.9.cloned.1.call-start = ((), (), s32[]{:S(2)}) async-start(), calls=%async_computation.9 | async-start | bytes 3538944 | tf_op jit(solution)/shard_map/reduce_scatter | solution.py:165
  224.9 7.6 copy-start.50
  224.9 7.6 copy-start.53
  262.5 10.2 %copy-start.54 = (bf16[768,1024]{1,0:T(8,128)(2,1)S(1)}, bf16[768,1024]{1,0:T(8,128)(2,1)}, u32[]{:S(2)}) copy-start(bf16[768,1024]{1,0:T(8,128)(2,1)} %param.24) | copy-start | bytes 4718596
  272.7 2.7 copy-start.59
  272.7 2.7 copy-start.61
  272.7 2.7 copy-start.55
  279.4 78.7 %all-gather.11.cloned.1.call-start = ((), (), s32[]{:S(2)}) async-start(), calls=%async_computation.10 | async-start | bytes 3538944 | tf_op jit(solution)/shard_map/all_gather | solution.py:178
  314.2 4.4 copy-start.6
  314.2 4.4 copy-start.9
  314.2 4.4 copy-start.10
  321.8 335.4 %reduce-scatter.11.cloned.1.call-start = ((), (), s32[]{:S(2)}) async-start(), calls=%async_computation.11 | async-start | bytes 3538944 | tf_op jit(solution)/shard_map/reduce_scatter | solution.py:234
  376.3 6.5 copy-start.1
  418.5 3.0 copy-start.2
  456.8 6.5 copy-start.1
  499.4 3.0 copy-start.2
  537.7 6.5 copy-start.1
  580.3 3.0 copy-start.2
  609.5 2.4 copy-start.4
  609.5 2.4 copy-start.19
  609.6 2.4 copy-start.21
  611.5 7.9 copy-start.13
  616.9 2.5 copy-start.11
  622.3 76.5 %reduce-scatter.7.cloned.1.call-start = ((), (), s32[]{:S(2)}) async-start(), calls=%async_computation.7 | async-start | bytes 3538944 | tf_op jit(solution)/shard_map/reduce_scatter | solution.py:150
  628.3 334.3 %all-reduce.5.cloned.1.call-start = ((), (), s32[]{:S(2)}) async-start(), calls=%async_computation.12 | async-start | bytes 28311552 | tf_op jit(solution)/shard_map/psum | solution.py:252
  628.6 7.2 copy-start.51
  628.6 7.2 copy-start.62
  635.8 4.4 copy-start.60
  640.2 4.4 copy-start.26
  640.2 4.4 copy-start.52
  649.1 2.4 copy-start.14
  654.0 3.2 copy-start.7
  654.0 3.2 copy-start.38
  654.0 3.2 copy-start.40
  654.0 5.6 copy-start.46
  654.1 44.8 %copy-start.34 = (f32[768]{0:T(1024)S(1)}, f32[768]{0:T(1024)}, u32[]{:S(2)}) copy-start(f32[768]{0:T(1024)} %copy-done.33) | copy-start | bytes 9220
  654.1 44.8 %copy-start.36 = (f32[768]{0:T(1024)S(1)}, f32[768]{0:T(1024)}, u32[]{:S(2)}) copy-start(f32[768]{0:T(1024)} %copy-done.35) | copy-start | bytes 9220
  654.1 44.8 %copy-start.42 = (f32[768]{0:T(1024)S(1)}, f32[768]{0:T(1024)}, u32[]{:S(2)}) copy-start(f32[768]{0:T(1024)} %copy-done.41) | copy-start | bytes 9220
  654.1 44.8 %copy-start.44 = (f32[768]{0:T(1024)S(1)}, f32[768]{0:T(1024)}, u32[]{:S(2)}) copy-start(f32[768]{0:T(1024)} %copy-done.43) | copy-start | bytes 9220
  654.1 44.8 %copy-start.45 = (f32[768]{0:T(1024)S(1)}, f32[768]{0:T(1024)}, u32[]{:S(2)}) copy-start(f32[768]{0:T(1024)} %get-tuple-element.284) | copy-start | bytes 9220
  962.6 2.5 copy-start.24
  962.6 3.5 copy-start.23
  966.1 2.8 copy-start.17
  969.0 3.0 copy-start.16
  972.0 3.0 copy-start.15
  (14 other events, 18.3 us)
Sparse Core Ops, SparseCore 0:
  13.7 38.7 all-gather.4
  150.1 34.7 reduce-scatter.4
  188.7 36.0 all-gather.6
  226.3 36.0 all-gather.8
  279.5 34.6 reduce-scatter.8
  321.9 36.0 all-gather.10
  622.5 34.7 reduce-scatter.10
  660.1 34.7 reduce-scatter.6
  701.5 261.0 all-reduce.4
